TPU v7x, 512 devices: a whole 4x4x16 slice. The times are simulated.
512 devices in a mesh: segment: 4 (over y_lo, core), band: 128 (over z, x, y_hi).
Axes of the slice: x: 4, y: 4 (y_hi: 2, y_lo: 2; y = y_hi * 2 + y_lo), z: 16, core: 2. Of those that a mesh axis runs over, the one named last changes fastest.
Arguments:
- voltages: bfloat16 [2, 2048, 16384], P(None, 'band', 'segment'), may hold values from -6 to 6
- slot_of_antenna: int32 [2048], replicated, may hold values from 0 to 2047, each once
- antenna_positions: int32 [2048, 2], replicated, may hold values from -1000 to 999
- beam_directions: int32 [1024, 2], replicated, may hold values from -64 to 63
Outputs:
- vis_real: float32 [128, 4, 256, 2048], P('band', 'segment')
- vis_imag: float32 [128, 4, 256, 2048], P('band', 'segment')
- beam_series: float32 [2, 4, 128, 2, 16384], P(None, 'segment', 'band')
Inputs may be any that keep to these rules, and one draw needn't show every extreme that they name: `slot_of_antenna`: a permutation of the antennas.
All inputs are finite; a program needn't handle non-finite values.
Results may differ from a plain program's by a relative error of at most 0.005.
Values may be sent and summed in bfloat16 or wider, within the bound.
A program may use at most 64 MiB of HBM per device.

v0:
```python
import math

import jax
import jax.numpy as jnp
from jax import lax
from jax.sharding import PartitionSpec as P

A = 2048
C = 64
BEAMS = 1024
NB = 256


def dft_parts():
    index = jnp.arange(64, dtype=jnp.int32)
    product = jnp.remainder(index[:, None] * index[None, :], 64).astype(jnp.float32)
    theta = product * (2.0 * math.pi / 64.0)
    return (jnp.cos(theta) * 0.125, jnp.sin(theta) * 0.125)


def forward_table():
    cosine, sine = dft_parts()
    return jnp.stack([jnp.stack([cosine, -sine], axis=1), jnp.stack([sine, cosine], axis=1)])


def inverse_table():
    cosine, sine = dft_parts()
    return jnp.stack([jnp.stack([cosine, sine], axis=1), jnp.stack([-sine, cosine], axis=1)])


def channelize(samples):
    count = samples.shape[2] // 64
    values = samples.astype(jnp.float32).reshape(2, samples.shape[1], count, 64)
    spectra = jnp.einsum(
        "pajn,pnqk->kqaj", values, forward_table(), precision=lax.Precision.HIGHEST
    )
    return spectra.astype(jnp.bfloat16)


def paired(spectra):
    doubled = jnp.broadcast_to(spectra[:, None], (spectra.shape[0], 2) + spectra.shape[1:])
    return doubled.reshape((2 * spectra.shape[0],) + spectra.shape[1:])


def steering(channel, directions, positions):
    delay = jnp.remainder(
        directions[:, 0:1] * positions[None, :, 0] + directions[:, 1:2] * positions[None, :, 1], 64
    )
    phase = jnp.remainder(channel * delay, 64).astype(jnp.float32) * (2.0 * math.pi / 64.0)
    return jnp.stack([jnp.cos(phase), -jnp.sin(phase)]).astype(jnp.bfloat16)


def resynthesize(received):
    lanes = received.shape[3]
    beams_here = received.shape[1]
    split = received.reshape(C, 2, beams_here, 2, lanes)
    series = jnp.einsum(
        "khbpj,pkqn->hbqjn", split, inverse_table(), precision=lax.Precision.HIGHEST
    )
    return series.reshape(2, beams_here, 2, lanes * 64)


def per_device(voltages, slot_of_antenna, antenna_positions, beam_directions):
    n_segment = lax.axis_size("segment")
    n_band = lax.axis_size("band")
    segment = lax.axis_index("segment")
    band = lax.axis_index("band")
    pair_count = 2 * C // n_band
    row_block = A // (2 * n_segment)
    beam_block = BEAMS // (2 * n_segment)
    beam_scale = 1.0 / math.sqrt(A)
    pair_ids = band * pair_count + jnp.arange(pair_count, dtype=jnp.int32)
    channels = pair_ids // 2
    halves = pair_ids % 2
    row_starts = (halves * n_segment + segment) * row_block
    beam_starts = halves * (n_segment * beam_block) + segment * beam_block

    def pair_weights(channel, beam_start):
        directions = lax.dynamic_slice_in_dim(beam_directions, beam_start, beam_block, 0)
        return steering(channel, directions, antenna_positions)

    weights = jax.vmap(pair_weights)(channels, beam_starts)

    def pair_terms(block, weight, row_start):
        rows = lax.dynamic_slice_in_dim(block, row_start, row_block, 1)
        turned = jnp.stack([rows[1], -rows[0]])
        left = jnp.stack([rows, turned])
        gram = jnp.einsum("gprt,pat->gra", left, block, preferred_element_type=jnp.float32)
        mixed = jnp.einsum("gba,pat->gbpt", weight, block, preferred_element_type=jnp.float32)
        formed_real = mixed[0, :, 0] - mixed[1, :, 1]
        formed_imag = mixed[0, :, 1] + mixed[1, :, 0]
        return (gram, jnp.stack([formed_real, formed_imag], axis=1) * beam_scale)

    spectra = paired(channelize(voltages))
    owned = lax.all_to_all(spectra, "band", split_axis=0, concat_axis=2, tiled=True)
    ordered = jnp.take(
        lax.all_gather(owned, "segment", axis=3, tiled=True), slot_of_antenna, axis=2
    )
    gram_part, formed_part = jax.vmap(pair_terms)(ordered, weights, row_starts)
    formed_total = formed_part
    gram_total, formed_total = (gram_part, formed_total)
    gram_total = gram_total * (1.0 / NB)
    vis_real = gram_total[:, 0][:, None]
    vis_imag = gram_total[:, 1][:, None]
    series = resynthesize(
        lax.all_to_all(
            formed_total.astype(jnp.bfloat16), "band", split_axis=1, concat_axis=0, tiled=True
        ).astype(formed_total.dtype)
    )
    beam_series = series.reshape(2, 1, series.shape[1], 2, series.shape[3])
    return (vis_real, vis_imag, beam_series)


def solution(mesh):
    in_specs = (P(None, "band", "segment"), P(), P(), P())
    out_specs = (
        P("band", "segment", None, None),
        P("band", "segment", None, None),
        P(None, "segment", "band", None, None),
    )
    return jax.shard_map(
        per_device, mesh=mesh, in_specs=in_specs, out_specs=out_specs, check_vma=False
    )
```

profile of v0, /device:TPU:1, one launch (start us, length us, event | category | flops | bytes accessed | tf_op | source)
XLA Modules:
  0.0 168.4 jit_solution(14214573905199428207)
XLA Ops:
  7.2 0.0 copy-start
  7.2 0.0 all-gather.2.cloned.1.call-start
  7.2 0.1 fusion.41
  7.4 0.2 sine_multiply_fusion
  7.5 1.5 reshape.623
  9.0 0.9 fusion.7
  9.9 0.3 copy.34
  10.3 0.2 broadcast_in_dim.34
  10.5 0.6 reshape.700
  11.1 50.4 %all_to_all.27 = bf16[128,2,1024]{2,1,0:T(2,128)(2,1)S(1)} all-to-all(bf16[128,2,1024]{2,1,0:T(2,128)(2,1)S(1)} %reshape.700), channel_id=1, replica_groups=mesh['segment'=4,'band'=128] {'band'}, dimensions={0} | all-to-all | bytes 1048576 | tf_op jit(solution)/shard_map/all_to_all | solution.py:95
  61.5 0.6 reshape.701
  62.1 0.0 copy-start.2
  62.1 0.0 copy-start.3
  62.2 0.2 copy.35
  62.3 1.3 copy.36
  63.7 0.0 all-gather.2.cloned.1.call-update
  63.8 0.0 copy-done.3
  63.8 5.0 %cosine_convert_fusion = (bf16[1,128,2048]{2,1,0:T(8,128)(2,1)S(1)}, bf16[1,128,2048]{2,1,0:T(8,128)(2,1)S(1)}) fusion(s32[2048]{0:T(1024)S(1)} %bitcast.117, s32[128]{0:T(128)S(1)} %get-tuple-element.51, s32[2048]{0:T(1024)S(1)} %bitcast.116, s32[128]{0:T(128)S(1)} %get-tuple-element.50, s32[]{:T(128)} %bitcast.30), kind=kLoop, calls=%fused_computation.31 | loop fusion | flops 8126464 | bytes 1065988 | tf_op jit(solution)/shard_map/convert
  68.8 28.5 %all-gather.2.cloned.1.call-done = bf16[1,2,2048,256]{2,1,0,3:T(2,128)(2,1)} async-done(((bf16[1,2,2048,64]{2,1,0,3:T(2,128)(2,1)}), bf16[1,2,2048,256]{2,1,0,3:T(2,128)(2,1)}) %all-gather.2.cloned.1.call-update) | async-done | bytes 2097168 | tf_op jit(solution)/shard_map/all_gather | solution.py:97
  97.3 8.3 %copy.37 = bf16[1,2,2048,256]{3,1,2,0:T(2,128)(2,1)S(1)} copy(bf16[1,2,2048,256]{2,1,0,3:T(2,128)(2,1)} %all-gather.2.cloned.1.call-done) | data formatting | bytes 4194304 | tf_op jit(solution)/shard_map/all_gather | solution.py:97
  105.6 16.5 %gather_fusion = bf16[2048,2,256]{2,1,0:T(2,128)(2,1)} fusion(bf16[2,2048,256]{2,0,1:T(2,128)(2,1)S(1)} %bitcast.110, s32[2048]{0:T(1024)S(1)} %fusion.42), kind=kCustom, calls=%fused_computation | custom fusion | bytes 4202496 | tf_op jit(solution)/shard_map/jit(_take)/gather | solution.py:96
  122.1 2.1 %bitcast_select_fusion = bf16[1,2,2048,256]{3,2,0,1:T(8,128)(2,1)S(1)} fusion(pred[2048]{0:T(1024)(128)(4,1)S(1)} %compare_and_fusion, bf16[2048,2,256]{2,1,0:T(2,128)(2,1)} %gather_fusion), kind=kLoop, calls=%fused_computation.3 | loop fusion | flops 1048576 | bytes 4196352 | tf_op jit(solution)/shard_map/jit(_take)/select_n | solution.py:96
  124.2 0.1 copy-done.1
  124.3 0.9 fusion.8
  125.2 0.8 copy.39
  126.0 18.7 %all-to-all-start.1 = ((bf16[1,128,2,256]{3,2,0,1:T(2,128)(2,1)}), bf16[1,128,2,256]{3,2,0,1:T(2,128)(2,1)S(1)}, u32[]{:S(2)}, u32[]{:S(2)}) async-start(bf16[1,128,2,256]{3,2,0,1:T(2,128)(2,1)} %copy.39), calls=%async_computation.1 | async-start | bytes 262144 | tf_op jit(solution)/shard_map/all_to_all | solution.py:106
  144.9 1.3 fusion
  146.2 2.3 %fusion.47 = (f32[1,1,256,2048]{3,2,1,0:T(8,128)}, f32[1,1,256,2048]{3,2,1,0:T(8,128)}) fusion(f32[1,2,256,2048]{3,2,1,0:T(8,128)S(1)} %fusion), kind=kLoop, calls=%fused_computation.84 | loop fusion | bytes 8388608 | tf_op jit(solution)/shard_map/slice | solution.py:104
  148.4 11.6 %all-to-all-done.1 = bf16[1,128,2,256]{3,2,0,1:T(2,128)(2,1)S(1)} async-done(((bf16[1,128,2,256]{3,2,0,1:T(2,128)(2,1)}), bf16[1,128,2,256]{3,2,0,1:T(2,128)(2,1)S(1)}, u32[]{:S(2)}, u32[]{:S(2)}) %all-to-all-start.1) | async-done | bytes 131104 | tf_op jit(solution)/shard_map/all_to_all | solution.py:106
  160.0 0.3 convolution_bitcast_fusion.1
  160.4 0.2 copy.42
  160.6 1.0 reshape_reshape.3
  (14 shorter events, 0.2 us)
Async XLA Ops:
  7.2 56.6 %copy-start = (s32[1024,2]{0,1:T(2,128)S(1)}, s32[1024,2]{0,1:T(2,128)}, u32[]{:S(2)}) copy-start(s32[1024,2]{0,1:T(2,128)} %param.7) | copy-start | bytes 24580
  7.2 90.1 %all-gather.2.cloned.1.call-start = ((), (), s32[]{:S(2)}) async-start(), calls=%async_computation.2 | async-start | bytes 2621440 | tf_op jit(solution)/shard_map/all_gather | solution.py:97
  62.1 1.6 copy-start.2
  62.1 1.7 copy-start.3
  122.1 2.2 %copy-start.1 = (bf16[2048,2,256]{2,1,0:T(2,128)(2,1)S(1)}, bf16[2048,2,256]{2,1,0:T(2,128)(2,1)}, u32[]{:S(2)}) copy-start(bf16[2048,2,256]{2,1,0:T(2,128)(2,1)} %gather_fusion) | copy-start | bytes 6291460
  126.0 34.0 %all-to-all-start.1 = ((bf16[1,128,2,256]{3,2,0,1:T(2,128)(2,1)}), bf16[1,128,2,256]{3,2,0,1:T(2,128)(2,1)S(1)}, u32[]{:S(2)}, u32[]{:S(2)}) async-start(bf16[1,128,2,256]{3,2,0,1:T(2,128)(2,1)} %copy.39), calls=%async_computation.1 | async-start | bytes 262144 | tf_op jit(solution)/shard_map/all_to_all | solution.py:106
Sparse Core Ops, SparseCore 0:
  63.8 33.4 all-gather.1
where the time goes:
time: 171 us; the launch traced here: 168 us
  blocking collectives  50.4 us (29%)
  waiting for transfers between devices  40.1 us (23%)
  local copies, waits for them, and re-layouts  33.9 us (20%)
  starting transfers between devices  18.8 us (11%)
  between operations  14.3 us (8%)
  other arithmetic  7.53 us (4%)
  matrix products  3.38 us (2%)
    all_to_all x1, blocking collectives, per_device(): lax.all_to_all(spectra, 'band', split_axis=0, concat_axis=2, tiled=True)  50.4 us
    all_gather x1, waiting for transfers between devices, per_device(): lax.all_gather(owned, 'segment', axis=3, tiled=True)  28.5 us
    all_to_all x1, starting transfers between devices, per_device(): lax.all_to_all(formed_total.astype(jnp.bfloat16), 'band', split_axis=1, c...  18.7 us
    gather x1, local copies, waits for them, and re-layouts, per_device(): jnp.take(lax.all_gather(owned, 'segment', axis=3, tiled=True), slot_of_an...  16.5 us
    all_to_all x1, waiting for transfers between devices, per_device(): lax.all_to_all(formed_total.astype(jnp.bfloat16), 'band', split_axis=1, c...  11.6 us
    all_gather x1, local copies, waits for them, and re-layouts, per_device(): lax.all_gather(owned, 'segment', axis=3, tiled=True)  8.26 us
    another operation x1, other arithmetic  4.98 us
  transfers between devices with their start and end apart: 2, of which 2 were waited for; matrix products, arithmetic and copies ran while one was open for 5% of the time, Pallas kernels for 0%

commit v1 on v0

v1 whole, which is shorter than its diff:
```python
import functools
import math

import jax
import jax.numpy as jnp
import numpy as np
from jax import lax
from jax.experimental import pallas as pl
from jax.experimental.pallas import tpu as pltpu
from jax.sharding import PartitionSpec as P

A = 2048
C = 64
BEAMS = 1024
NB = 256
MESH = pl.DeviceIdType.MESH


def dft_parts():
    index = np.arange(64)
    theta = (np.outer(index, index) % 64) * (2.0 * math.pi / 64.0)
    return np.cos(theta) * 0.125, np.sin(theta) * 0.125


def split(table):
    high = table.astype(np.float32).astype(jnp.bfloat16)
    low = (table - high.astype(np.float64)).astype(np.float32).astype(jnp.bfloat16)
    return high, low


def forward_tables():
    cosine, sine = dft_parts()
    parts = np.array([[cosine, -sine], [sine, cosine]])
    table = np.zeros((2, 2, 64, 2, 2, 64))
    for t1 in range(2):
        table[:, t1, :, :, t1, :] = parts.transpose(1, 3, 0, 2)
    return split(table.reshape(256, 256))


def inverse_table():
    cosine, sine = dft_parts()
    return np.array([[cosine, sine], [-sine, cosine]]).transpose(0, 2, 1, 3)


def steering_table():
    phase = np.arange(64) * (2.0 * math.pi / 64.0)
    row = np.concatenate([np.cos(phase), -np.sin(phase)]).astype(np.float32)
    return np.broadcast_to(row, (128, 128))


def place():
    segment = lax.axis_index("segment")
    band = lax.axis_index("band")
    core, half, channel = segment % 2, band % 2, band // 2
    return segment, band, core, half, channel, channel // 4, channel % 4, half * 2 + segment // 2


def offset_of(step):
    odd = step % 2
    return (8 + odd * (-(step + 1) // 2) + (1 - odd) * (step // 2)) % 16


def channelize(v_ref, high_ref, low_ref, wide, turned, spectra_f, spectra):
    for p in range(2):
        for t2 in range(32):
            wide[p, t2 * 16 : (t2 + 1) * 16, :] = v_ref[p, :, t2 * 128 : (t2 + 1) * 128].astype(
                jnp.float32
            )
    for a in range(16):
        for p in range(2):
            turned[a * 32 : (a + 1) * 32, p * 128 : (p + 1) * 128] = wide[
                p, pl.ds(a, 32, stride=16), :
            ].astype(jnp.bfloat16)
    dims = (((1,), (1,)), ((), ()))
    lane = lax.broadcasted_iota(jnp.int32, (64, 128), 1)
    first, even = lane < 64, (lane // 32) % 2 == 0
    for g in range(4):
        block = turned[g * 128 : (g + 1) * 128, :]
        out = lax.dot_general(high_ref[...], block, dims, preferred_element_type=jnp.float32)
        out += lax.dot_general(low_ref[...], block, dims, preferred_element_type=jnp.float32)
        part = [out[i * 64 : (i + 1) * 64] for i in range(4)]
        for i in range(2):
            a, b = part[i], part[i + 2]
            part[i] = jnp.where(first, a, pltpu.roll(b, 64, 1))
            part[i + 2] = jnp.where(first, pltpu.roll(a, 64, 1), b)
        for i in (0, 2):
            a, b = part[i], part[i + 1]
            part[i] = jnp.where(even, a, pltpu.roll(b, 32, 1))
            part[i + 1] = jnp.where(even, pltpu.roll(a, 96, 1), b)
        for i in range(4):
            spectra_f[pl.ds(g * 4 + i, 64, stride=16), :] = part[i]
    spectra[...] = spectra_f[...].astype(jnp.bfloat16)


def gather_kernel(
    v_ref, high_ref, low_ref, x_ref,
    wide, turned, spectra_f, spectra,
    send_a, recv_a, own_sem, send_y, recv_y, send_c, recv_c,
):
    segment, band, core, half, channel, z, x, y = place()

    def column(y_to, core_to):
        return ((y_to % 2) * 2 + core_to, channel * 2 + y_to // 2)

    up, down = (y + 1) % 4, (y + 3) % 4
    partner = column(y, 1 - core)
    barrier = pltpu.get_barrier_semaphore()

    def greet(step, carry):
        other = (channel + step) % 64
        pl.semaphore_signal(
            barrier, inc=1, device_id=(segment, other * 2 + half), device_id_type=MESH
        )
        return carry

    lax.fori_loop(1, 64, greet, 0)
    for target in (column(up, core), column(down, core), partner):
        pl.semaphore_signal(barrier, inc=1, device_id=target, device_id_type=MESH)

    channelize(v_ref, high_ref, low_ref, wide, turned, spectra_f, spectra)

    pl.semaphore_wait(barrier, 66)

    def chunk(y_from, core_from, z_from, rows):
        row = pl.multiple_of((y_from // 2) * 1024 + z_from * 64, 64)
        lane = pl.multiple_of(((y_from % 2) * 2 + core_from) * 128, 128)
        return x_ref.at[pl.ds(row, rows), pl.ds(lane, 128)]

    home = x_ref.at[
        pl.ds(pl.multiple_of(half * 1024 + channel * 16, 16), 16),
        pl.ds(pl.multiple_of(segment * 128, 128), 128),
    ]

    def message(step, across):
        to = ((z + offset_of(step)) % 16) * 4 + (x + across) % 4
        return pltpu.make_async_remote_copy(
            src_ref=spectra.at[pl.ds(pl.multiple_of(to * 16, 16), 16), :],
            dst_ref=home,
            send_sem=send_a,
            recv_sem=recv_a.at[step],
            device_id=(segment, to * 2 + half),
            device_id_type=MESH,
        )

    def send(step, carry):
        for across in range(4):
            message(step, across).start()
        return carry

    lax.fori_loop(0, 15, send, 0)
    for across in range(1, 4):
        message(15, across).start()
    own = pltpu.make_async_copy(
        spectra.at[pl.ds(pl.multiple_of(channel * 16, 16), 16), :], home, own_sem
    )
    own.start()

    def forward(y_from, step, target, send_sem, recv_sem):
        source = chunk(y_from, core, (z + 16 - offset_of(step)) % 16, 64)
        return pltpu.make_async_remote_copy(
            src_ref=source,
            dst_ref=source,
            send_sem=send_sem,
            recv_sem=recv_sem,
            device_id=target,
            device_id_type=MESH,
        )

    relay_from = (y + 3 + 2 * core) % 4
    relay_to = (y + 1 + 2 * core) % 4
    across_from = (y + 2) % 4

    def arrived(ref, sem):
        pltpu.make_async_copy(ref, ref, sem).wait()

    def to_partner(y_from, kind, step):
        forward(y_from, step, partner, send_c.at[kind], recv_c.at[kind]).start()

    def level0(step):
        forward(y, step, column(up, core), send_y.at[0], recv_y.at[0, step]).start()
        forward(y, step, column(down, core), send_y.at[1], recv_y.at[1, step]).start()
        to_partner(y, 0, step)

    def level1(step):
        first = forward(down, step, partner, send_y.at[0], recv_y.at[0, step])
        second = forward(up, step, partner, send_y.at[1], recv_y.at[1, step])
        first.wait_recv()
        second.wait_recv()
        forward(relay_from, step, column(relay_to, core), send_y.at[2], recv_y.at[2, step]).start()
        to_partner(down, 1, step)
        to_partner(up, 2, step)

    def level2(step):
        forward(across_from, step, partner, send_y.at[2], recv_y.at[2, step]).wait_recv()
        to_partner(across_from, 3, step)

    def wait_level0(step):
        z_from = (z + 16 - offset_of(step)) % 16
        arrived(chunk(y, core, z_from, 64), recv_a.at[step])

    wait_level0(0)
    level0(0)
    wait_level0(1)
    level0(1)
    level1(0)

    def body(step, carry):
        wait_level0(step)
        level0(step)
        level1(step - 1)
        level2(step - 2)
        return carry

    lax.fori_loop(2, 15, body, 0)
    own.wait()
    arrived(x_ref.at[pl.ds(0, 48), pl.ds(0, 128)], recv_a.at[15])
    level0(15)
    level1(14)
    level2(13)
    level1(15)
    level2(14)
    level2(15)

    def plane(y_from, core_from):
        return chunk(y_from, core_from, 0, 1024)

    for kind, y_from in enumerate((y, down, up, across_from)):
        arrived(plane(y_from, 1 - core), recv_c.at[kind])
        arrived(plane(y_from, core), send_c.at[kind])
    for kind in range(3):
        arrived(plane(y, core), send_y.at[kind])
    arrived(spectra.at[pl.ds(0, 63 * 16), :], send_a)


def column_of(row):
    return jnp.transpose(jnp.broadcast_to(row, (128, 128)))


def local_kernel(
    x_ref, slot_ref, pos_ref, dir_ref, tab_ref, real_ref, imag_ref, formed_ref,
    pick, weight_a, weight_u, ordered, left,
):
    segment, band, core, half, channel, z, x, y = place()

    lane = lax.broadcasted_iota(jnp.int32, (128, 128), 1)
    for r in range(16):
        slot = column_of(slot_ref[r : r + 1, :])
        for c in range(16):
            position = lane + c * 128
            name = ((position % 1024) // 16) * 32 + (position // 1024) * 16 + position % 16
            pick[r * 128 : (r + 1) * 128, c * 128 : (c + 1) * 128] = jnp.where(
                slot == name, 1.0, 0.0
            ).astype(jnp.bfloat16)

    start = pl.multiple_of(half * 512 + segment * 128, 128)
    turn0 = column_of(dir_ref[0:1, pl.ds(start, 128)]) * channel
    turn1 = column_of(dir_ref[1:2, pl.ds(start, 128)]) * channel
    table = tab_ref[...]
    for c in range(16):
        sl = slice(c * 128, (c + 1) * 128)
        phase = (turn0 * pos_ref[0:1, sl] + turn1 * pos_ref[1:2, sl]) & 63
        weight_a[0:128, sl] = jnp.take_along_axis(table, phase, axis=1).astype(jnp.bfloat16)
        weight_a[128:256, sl] = jnp.take_along_axis(table, phase + 64, axis=1).astype(jnp.bfloat16)

    for c in range(8):
        sl = slice(c * 256, (c + 1) * 256)
        weight_u[:, sl] = jnp.dot(
            weight_a[...], pick[:, sl], preferred_element_type=jnp.float32
        ).astype(jnp.bfloat16)

    low_lane = lax.broadcasted_iota(jnp.int32, (128, 128), 1) < 64
    beam_scale = 1.0 / math.sqrt(A)
    mixed = jnp.dot(weight_u[...], x_ref[...], preferred_element_type=jnp.float32)
    for s in range(4):
        sl = slice(s * 128, (s + 1) * 128)
        other = pltpu.roll(mixed[128:256, sl], 64, 1)
        formed = mixed[0:128, sl] + jnp.where(low_lane, -other, other)
        formed_ref[:, sl] = (formed * beam_scale).astype(jnp.bfloat16)

    def reorder(step, carry):
        rows = pl.ds(pl.multiple_of(step * 256, 256), 256)
        ordered[rows, :] = jnp.dot(
            pick[rows, :], x_ref[...], preferred_element_type=jnp.float32
        ).astype(jnp.bfloat16)
        return carry

    lax.fori_loop(0, 8, reorder, 0)

    mine = ordered[pl.ds(pl.multiple_of((half * 4 + segment) * 256, 256), 256), :]
    low_lanes = lax.broadcasted_iota(jnp.int32, (256, 128), 1) < 64
    left[0:256, :] = mine
    for s in range(4):
        sl = slice(s * 128, (s + 1) * 128)
        other = pltpu.roll(mine[:, sl].astype(jnp.float32), 64, 1)
        left[256:512, sl] = jnp.where(low_lanes, other, -other).astype(jnp.bfloat16)
    dims = (((1,), (1,)), ((), ()))
    for b in range(8):
        sl = slice(b * 256, (b + 1) * 256)
        gram = lax.dot_general(left[...], ordered[sl, :], dims, preferred_element_type=jnp.float32)
        gram = gram * (1.0 / NB)
        real_ref[:, sl] = gram[0:256]
        imag_ref[:, sl] = gram[256:512]


VMEM = pl.BlockSpec(memory_space=pltpu.VMEM)


def per_device(voltages, slot_of_antenna, antenna_positions, beam_directions):
    high, low = forward_tables()
    spectra = pl.pallas_call(
        gather_kernel,
        out_shape=jax.ShapeDtypeStruct((A, 512), jnp.bfloat16),
        in_specs=[VMEM] * 3,
        out_specs=VMEM,
        scratch_shapes=[
            pltpu.VMEM((2, 512, 128), jnp.float32),
            pltpu.VMEM((512, 256), jnp.bfloat16),
            pltpu.VMEM((1024, 128), jnp.float32),
            pltpu.VMEM((1024, 128), jnp.bfloat16),
            pltpu.SemaphoreType.DMA,
            pltpu.SemaphoreType.DMA((16,)),
            pltpu.SemaphoreType.DMA,
            pltpu.SemaphoreType.DMA((3,)),
            pltpu.SemaphoreType.DMA((3, 16)),
            pltpu.SemaphoreType.DMA((4,)),
            pltpu.SemaphoreType.DMA((4,)),
        ],
        compiler_params=pltpu.CompilerParams(collective_id=0, has_side_effects=True),
        name="exchange",
    )(voltages, jnp.asarray(high), jnp.asarray(low))
    real, imag, formed = pl.pallas_call(
        local_kernel,
        out_shape=(
            jax.ShapeDtypeStruct((256, A), jnp.float32),
            jax.ShapeDtypeStruct((256, A), jnp.float32),
            jax.ShapeDtypeStruct((128, 512), jnp.bfloat16),
        ),
        in_specs=[VMEM] * 5,
        out_specs=(VMEM, VMEM, VMEM),
        scratch_shapes=[
            pltpu.VMEM((A, A), jnp.bfloat16),
            pltpu.VMEM((256, A), jnp.bfloat16),
            pltpu.VMEM((256, A), jnp.bfloat16),
            pltpu.VMEM((A, 512), jnp.bfloat16),
            pltpu.VMEM((512, 512), jnp.bfloat16),
        ],
        compiler_params=pltpu.CompilerParams(vmem_limit_bytes=50 * 2**20),
        name="local",
    )(
        spectra,
        slot_of_antenna.reshape(16, 128),
        antenna_positions.T,
        beam_directions.T,
        jnp.asarray(steering_table()),
    )
    received = lax.all_to_all(formed, "band", split_axis=0, concat_axis=0, tiled=True)
    split_up = received.reshape(C, 2, 4, 2, 2, 32).astype(jnp.float32)
    series = jnp.einsum(
        "khsqrt,qkpn->hpstrn",
        split_up,
        jnp.asarray(inverse_table(), jnp.float32),
        precision=lax.Precision.HIGHEST,
    )
    return (real[None, None], imag[None, None], series.reshape(2, 1, 1, 2, NB * 64))


def solution(mesh):
    in_specs = (P(None, "band", "segment"), P(), P(), P())
    out_specs = (
        P("band", "segment", None, None),
        P("band", "segment", None, None),
        P(None, "segment", "band", None, None),
    )
    return jax.shard_map(
        per_device, mesh=mesh, in_specs=in_specs, out_specs=out_specs, check_vma=False
    )
```

time: 171 us -> 123 us (0.72)
  the two profiles are of different devices: /device:TPU:1 before, /device:TPU:32 now
where the time goes in v1:
time: 123 us; the launch traced here: 122 us
  Pallas kernels  82.8 us (67%)
  blocking collectives  32.7 us (27%)
  local copies, waits for them, and re-layouts  4.13 us (3%)
  other arithmetic  1.43 us (1%)
    pallas_call x1, Pallas kernels, per_device(): pl.pallas_call(gather_kernel, out_shape=jax.ShapeDtypeStruct((A, 512), jn...  69.2 us
    all_to_all x1, blocking collectives, per_device(): lax.all_to_all(formed, 'band', split_axis=0, concat_axis=0, tiled=True)  32.7 us
    pallas_call x1, Pallas kernels, per_device(): pl.pallas_call(local_kernel, out_shape=(jax.ShapeDtypeStruct((256, A), jn...  13.6 us

profile of v1, /device:TPU:32, one launch (start us, length us, event | category | flops | bytes accessed | tf_op | source)
XLA Modules:
  0.0 122.5 jit_solution(4797713036910299973)
XLA Ops:
  0.6 0.0 copy-start.5
  0.6 0.0 copy-start.2
  0.7 0.0 copy-start.1
  0.7 0.0 copy-start.3
  0.7 69.2 %exchange.1.x_ref = bf16[2048,512]{1,0:T(8,128)(2,1)} custom-call(bf16[2,16,4096]{2,1,0:T(8,128)(2,1)} %v_ref.1, bf16[256,256]{1,0:T(8,128)(2,1)} %constant.8.clone.high_ref, bf16[256,256]{1,0:T(8,128)(2,1)} %constant.9.clone.low_ref), custom_call_target="tpu_custom_call" | custom-call | tf_op jit(solution)/shard_map/exchange/pallas_call | solution.py:310
  69.9 0.0 copy-done.5
  69.9 0.0 copy-done.2
  69.9 0.0 copy-done.1
  69.9 0.0 copy-done.3
  69.9 0.0 copy-start
  69.9 1.6 %copy-done = bf16[2048,512]{1,0:T(8,128)(2,1)S(1)} copy-done((bf16[2048,512]{1,0:T(8,128)(2,1)S(1)}, bf16[2048,512]{1,0:T(8,128)(2,1)}, u32[]{:S(2)}) %copy-start) | copy-done | bytes 2097176
  71.5 0.0 copy-start.4
  71.5 13.6 %local.1 = (f32[256,2048]{1,0:T(8,128)}, f32[256,2048]{1,0:T(8,128)}, bf16[128,512]{1,0:T(8,128)(2,1)S(1)}) custom-call(bf16[2048,512]{1,0:T(8,128)(2,1)S(1)} %copy-done, s32[16,128]{1,0:T(8,128)S(1)} %bitcast.19, s32[2,2048]{1,0:T(2,128)S(1)} %bitcast.18, s32[2,1024]{1,0:T(2,128)S(1)} %bitcast.20, f32[128,128]{1,0:T(8,128)S(1)} %jit_solution_.3.tab_ref), custom_call_target="tpu_custom_call" | custom-call | tf_op jit(solution)/shard_map/local/pallas_call | solution.py:331
  85.1 0.5 broadcast.1
  85.6 0.7 reduce.1
  86.3 32.7 %all_to_all.9 = bf16[128,2,256]{2,1,0:T(2,128)(2,1)S(1)} all-to-all(bf16[128,2,256]{2,1,0:T(2,128)(2,1)S(1)} %reshape.25), channel_id=1, replica_groups=mesh['segment'=4,'band'=128] {'band'}, dimensions={0} | all-to-all | bytes 262144 | tf_op jit(solution)/shard_map/all_to_all | solution.py:356
  119.1 0.1 reshape.26
  119.2 0.8 reduce
  119.9 0.3 reshape.19
  120.2 0.0 copy-done.4
  120.2 0.6 convolution_bitcast_fusion
  120.9 0.4 copy.17
  121.3 1.2 reshape.20
  (2 shorter events, 0.0 us)
Async XLA Ops:
  0.6 69.2 %copy-start.5 = (f32[128]{0:T(128)S(1)}, f32[128]{0:T(128)}, u32[]{:S(2)}) copy-start(f32[128]{0:T(128)} %constant.10.clone) | copy-start | bytes 1540
  0.6 69.2 %copy-start.2 = (s32[2048]{0:T(1024)S(1)}, s32[2048]{0:T(1024)}, u32[]{:S(2)}) copy-start(s32[2048]{0:T(1024)} %param.9) | copy-start | bytes 24580
  0.7 69.2 %copy-start.1 = (s32[2048,2]{0,1:T(2,128)S(1)}, s32[2048,2]{0,1:T(2,128)}, u32[]{:S(2)}) copy-start(s32[2048,2]{0,1:T(2,128)} %param.10) | copy-start | bytes 49156
  0.7 69.2 %copy-start.3 = (s32[1024,2]{0,1:T(2,128)S(1)}, s32[1024,2]{0,1:T(2,128)}, u32[]{:S(2)}) copy-start(s32[1024,2]{0,1:T(2,128)} %param.11) | copy-start | bytes 24580
  69.9 1.6 %copy-start = (bf16[2048,512]{1,0:T(8,128)(2,1)S(1)}, bf16[2048,512]{1,0:T(8,128)(2,1)}, u32[]{:S(2)}) copy-start(bf16[2048,512]{1,0:T(8,128)(2,1)} %exchange.1.x_ref) | copy-start | bytes 6291460
  71.5 48.7 %copy-start.4 = (f32[2,64,2,64,1,1,1]{3,1,0,2,6,5,4:T(8,128)S(1)}, f32[2,64,2,64,1,1,1]{3,1,0,2,6,5,4:T(8,128)}, u32[]{:S(2)}) copy-start(f32[2,64,2,64,1,1,1]{3,1,0,2,6,5,4:T(8,128)} %constant.13) | copy-start | bytes 196612

commit v2 on v1

v2 whole, which is shorter than its diff:
```python
import math

import jax
import jax.numpy as jnp
import numpy as np
from jax import lax
from jax.experimental import pallas as pl
from jax.experimental.pallas import tpu as pltpu
from jax.sharding import PartitionSpec as P

A = 2048
C = 64
BEAMS = 1024
NB = 256
MESH = pl.DeviceIdType.MESH
LAG = 5


def dft_parts():
    index = np.arange(64)
    theta = (np.outer(index, index) % 64) * (2.0 * math.pi / 64.0)
    return np.cos(theta) * 0.125, np.sin(theta) * 0.125


def split(table):
    high = table.astype(np.float32).astype(jnp.bfloat16)
    low = (table - high.astype(np.float64)).astype(np.float32).astype(jnp.bfloat16)
    return high, low


def forward_tables():
    cosine, sine = dft_parts()
    parts = np.array([[cosine, -sine], [sine, cosine]])
    table = np.zeros((2, 2, 64, 2, 2, 64))
    for t1 in range(2):
        table[:, t1, :, :, t1, :] = parts.transpose(1, 3, 0, 2)
    return split(table.reshape(256, 256))


def inverse_tables():
    cosine, sine = dft_parts()
    parts = np.array([[cosine, sine], [-sine, cosine]])
    table = np.zeros((2, 2, 64, 2, 2, 64))
    for t1 in range(2):
        table[:, t1, :, :, t1, :] = parts.transpose(0, 2, 1, 3)
    return split(table.reshape(256, 256))


def steering_table():
    phase = np.arange(64) * (2.0 * math.pi / 64.0)
    row = np.concatenate([np.cos(phase), -np.sin(phase)]).astype(np.float32)
    return row.reshape(1, 128)


def place():
    segment = lax.axis_index("segment")
    band = lax.axis_index("band")
    core, half, channel = segment % 2, band % 2, band // 2
    return segment, band, core, half, channel, channel // 4, channel % 4, half * 2 + segment // 2


def offset_of(step):
    odd = step % 2
    return (8 + odd * (-(step + 1) // 2) + (1 - odd) * (step // 2)) % 16


def channelize(v_ref, high_ref, low_ref, wide, turned, spectra_f, spectra):
    for p in range(2):
        for t2 in range(32):
            wide[p, t2 * 16 : (t2 + 1) * 16, :] = v_ref[p, :, t2 * 128 : (t2 + 1) * 128].astype(
                jnp.float32
            )
    for a in range(16):
        for p in range(2):
            turned[a * 32 : (a + 1) * 32, p * 128 : (p + 1) * 128] = wide[
                p, pl.ds(a, 32, stride=16), :
            ].astype(jnp.bfloat16)
    dims = (((1,), (1,)), ((), ()))
    lane = lax.broadcasted_iota(jnp.int32, (64, 128), 1)
    first, even = lane < 64, (lane // 32) % 2 == 0
    for g in range(4):
        block = turned[g * 128 : (g + 1) * 128, :]
        out = lax.dot_general(high_ref[...], block, dims, preferred_element_type=jnp.float32)
        out += lax.dot_general(low_ref[...], block, dims, preferred_element_type=jnp.float32)
        part = [out[i * 64 : (i + 1) * 64] for i in range(4)]
        for i in range(2):
            a, b = part[i], part[i + 2]
            part[i] = jnp.where(first, a, pltpu.roll(b, 64, 1))
            part[i + 2] = jnp.where(first, pltpu.roll(a, 64, 1), b)
        for i in (0, 2):
            a, b = part[i], part[i + 1]
            part[i] = jnp.where(even, a, pltpu.roll(b, 32, 1))
            part[i + 1] = jnp.where(even, pltpu.roll(a, 96, 1), b)
        for i in range(4):
            spectra_f[pl.ds(g * 4 + i, 64, stride=16), :] = part[i]
    spectra[...] = spectra_f[...].astype(jnp.bfloat16)


def column_of(row):
    return jnp.transpose(jnp.broadcast_to(row, (128, 128)))


def build_pick(slot_ref, pick):
    lane = lax.broadcasted_iota(jnp.int32, (128, 128), 1)

    def block(r, carry):
        slot = column_of(slot_ref[pl.ds(r, 1), :])
        rows = pl.ds(pl.multiple_of(r * 128, 128), 128)
        for c in range(16):
            position = lane + c * 128
            name = ((position % 1024) // 16) * 32 + (position // 1024) * 16 + position % 16
            pick[rows, c * 128 : (c + 1) * 128] = jnp.where(slot == name, 1.0, 0.0).astype(
                jnp.bfloat16
            )
        return carry

    lax.fori_loop(0, 16, block, 0)


def build_weights(pos_ref, dir_ref, tab_ref, weight_a, half, segment, channel):
    start = pl.multiple_of(half * 512 + segment * 128, 128)
    turn0 = column_of(dir_ref[0:1, pl.ds(start, 128)]) * channel
    turn1 = column_of(dir_ref[1:2, pl.ds(start, 128)]) * channel
    table = jnp.broadcast_to(tab_ref[...], (128, 128))
    for c in range(16):
        sl = slice(c * 128, (c + 1) * 128)
        phase = (turn0 * pos_ref[0:1, sl] + turn1 * pos_ref[1:2, sl]) & 63
        weight_a[0:128, sl] = jnp.take_along_axis(table, phase, axis=1).astype(jnp.bfloat16)
        weight_a[128:256, sl] = jnp.take_along_axis(table, phase + 64, axis=1).astype(jnp.bfloat16)


def kernel(
    v_hbm, high_hbm, low_hbm, slot_hbm, pos_hbm, dir_hbm, tab_hbm,
    real_ref, imag_ref, beams_ref,
    v_ref, high_ref, low_ref, slot_ref, pos_ref, dir_ref, tab_ref,
    wide, turned, spectra_f, spectra, x_ref, pick, weight_a, weight_u, ordered, left,
    formed_f, formed,
    send_a, recv_a, send_y, recv_y, send_c, recv_c, send_b, recv_b, own_b, load,
):
    segment, band, core, half, channel, z, x, y = place()
    loads = [
        pltpu.make_async_copy(source, target, load.at[i])
        for i, (source, target) in enumerate(
            (
                (v_hbm, v_ref),
                (high_hbm, high_ref),
                (low_hbm, low_ref),
                (slot_hbm, slot_ref),
                (pos_hbm, pos_ref),
                (dir_hbm, dir_ref),
                (tab_hbm, tab_ref),
            )
        )
    ]
    for copy in loads:
        copy.start()

    def column(y_to, core_to):
        return ((y_to % 2) * 2 + core_to, channel * 2 + y_to // 2)

    up, down = (y + 1) % 4, (y + 3) % 4
    partner = column(y, 1 - core)
    barrier = pltpu.get_barrier_semaphore()

    def greet(step, carry):
        pl.semaphore_signal(
            barrier, inc=1, device_id=(segment, (band + step) % 128), device_id_type=MESH
        )
        return carry

    lax.fori_loop(1, 128, greet, 0)
    for target in (column(up, core), column(down, core), partner):
        pl.semaphore_signal(barrier, inc=1, device_id=target, device_id_type=MESH)

    for copy in loads:
        copy.wait()
    channelize(v_ref, high_ref, low_ref, wide, turned, spectra_f, spectra)
    build_pick(slot_ref, pick)
    build_weights(pos_ref, dir_ref, tab_ref, weight_a, half, segment, channel)

    pl.semaphore_wait(barrier, 130)

    def chunk(y_from, core_from, z_from, rows):
        row = pl.multiple_of((y_from // 2) * 1024 + z_from * 64, 64)
        lane = pl.multiple_of(((y_from % 2) * 2 + core_from) * 128, 128)
        return x_ref.at[pl.ds(row, rows), pl.ds(lane, 128)]

    home = x_ref.at[
        pl.ds(pl.multiple_of(half * 1024 + channel * 16, 16), 16),
        pl.ds(pl.multiple_of(segment * 128, 128), 128),
    ]

    def message(step, across):
        to = ((z + offset_of(step)) % 16) * 4 + (x + across) % 4
        return pltpu.make_async_remote_copy(
            src_ref=spectra.at[pl.ds(pl.multiple_of(to * 16, 16), 16), :],
            dst_ref=home,
            send_sem=send_a,
            recv_sem=recv_a.at[step],
            device_id=(segment, to * 2 + half),
            device_id_type=MESH,
        )

    def send(step, carry):
        for across in range(4):
            message(step, across).start()
        return carry

    lax.fori_loop(0, 15, send, 0)
    for across in range(1, 4):
        message(15, across).start()
    own = pltpu.make_async_copy(
        spectra.at[pl.ds(pl.multiple_of(channel * 16, 16), 16), :], home, recv_a.at[15]
    )
    own.start()

    def to_slots(c, carry):
        lanes = pl.ds(pl.multiple_of(c * 256, 256), 256)
        weight_u[:, lanes] = jnp.dot(
            weight_a[...], pick[:, lanes], preferred_element_type=jnp.float32
        ).astype(jnp.bfloat16)
        return carry

    lax.fori_loop(0, 8, to_slots, 0)

    def forward(y_from, step, target, send_sem, recv_sem):
        source = chunk(y_from, core, (z + 16 - offset_of(step)) % 16, 64)
        return pltpu.make_async_remote_copy(
            src_ref=source,
            dst_ref=source,
            send_sem=send_sem,
            recv_sem=recv_sem,
            device_id=target,
            device_id_type=MESH,
        )

    relay_from = (y + 3 + 2 * core) % 4
    relay_to = (y + 1 + 2 * core) % 4
    across_from = (y + 2) % 4

    def arrived(ref, sem):
        pltpu.make_async_copy(ref, ref, sem).wait()

    def to_partner(y_from, kind, step):
        forward(y_from, step, partner, send_c.at[kind], recv_c.at[kind]).start()

    def level0(step):
        arrived(chunk(y, core, (z + 16 - offset_of(step)) % 16, 64), recv_a.at[step])
        forward(y, step, column(up, core), send_y.at[0], recv_y.at[0, step]).start()
        forward(y, step, column(down, core), send_y.at[1], recv_y.at[1, step]).start()
        to_partner(y, 0, step)

    def level1(step):
        forward(down, step, partner, send_y.at[0], recv_y.at[0, step]).wait_recv()
        forward(up, step, partner, send_y.at[1], recv_y.at[1, step]).wait_recv()
        forward(relay_from, step, column(relay_to, core), send_y.at[2], recv_y.at[2, step]).start()
        to_partner(down, 1, step)
        to_partner(up, 2, step)

    def level2(step):
        forward(across_from, step, partner, send_y.at[2], recv_y.at[2, step]).wait_recv()
        to_partner(across_from, 3, step)

    def body(step, carry):
        pl.when(step < 16)(lambda: level0(step))
        pl.when((step >= LAG) & (step < 16 + LAG))(lambda: level1(step - LAG))
        pl.when(step >= 2 * LAG)(lambda: level2(step - 2 * LAG))
        return carry

    lax.fori_loop(0, 16 + 2 * LAG, body, 0)

    def plane(y_from, core_from):
        return chunk(y_from, core_from, 0, 1024)

    for kind, y_from in enumerate((y, down, up, across_from)):
        arrived(plane(y_from, 1 - core), recv_c.at[kind])

    low_lane = lax.broadcasted_iota(jnp.int32, (128, 128), 1) < 64
    beam_scale = 1.0 / math.sqrt(A)
    mixed = jnp.dot(weight_u[...], x_ref[...], preferred_element_type=jnp.float32)
    for s in range(4):
        sl = slice(s * 128, (s + 1) * 128)
        other = pltpu.roll(mixed[128:256, sl], 64, 1)
        sums = mixed[0:128, sl] + jnp.where(low_lane, -other, other)
        formed_f[pl.ds(s, 128, stride=4), :] = sums * beam_scale
    for e in range(128):
        formed[e] = formed_f[e * 4 : (e + 1) * 4, :].astype(jnp.bfloat16)

    def send_beams(step, carry):
        to = (band + 64 + step) % 128
        pltpu.make_async_remote_copy(
            src_ref=formed.at[to],
            dst_ref=beams_ref.at[band],
            send_sem=send_b,
            recv_sem=recv_b,
            device_id=(segment, to),
            device_id_type=MESH,
        ).start()
        return carry

    lax.fori_loop(0, 64, send_beams, 0)
    lax.fori_loop(65, 128, send_beams, 0)
    own_beam = pltpu.make_async_copy(formed.at[band], beams_ref.at[band], own_b)
    own_beam.start()

    def reorder(step, carry):
        rows = pl.ds(pl.multiple_of(step * 256, 256), 256)
        ordered[rows, :] = jnp.dot(
            pick[rows, :], x_ref[...], preferred_element_type=jnp.float32
        ).astype(jnp.bfloat16)
        return carry

    lax.fori_loop(0, 8, reorder, 0)

    mine = ordered[pl.ds(pl.multiple_of((half * 4 + segment) * 256, 256), 256), :]
    low_lanes = lax.broadcasted_iota(jnp.int32, (256, 128), 1) < 64
    left[0:256, :] = mine
    for s in range(4):
        sl = slice(s * 128, (s + 1) * 128)
        other = pltpu.roll(mine[:, sl].astype(jnp.float32), 64, 1)
        left[256:512, sl] = jnp.where(low_lanes, other, -other).astype(jnp.bfloat16)
    dims = (((1,), (1,)), ((), ()))

    def correlate(step, carry):
        rows = pl.ds(pl.multiple_of(step * 256, 256), 256)
        gram = lax.dot_general(left[...], ordered[rows, :], dims, preferred_element_type=jnp.float32)
        gram = gram * (1.0 / NB)
        real_ref[:, rows] = gram[0:256]
        imag_ref[:, rows] = gram[256:512]
        return carry

    lax.fori_loop(0, 8, correlate, 0)

    for kind, y_from in enumerate((y, down, up, across_from)):
        arrived(plane(y_from, core), send_c.at[kind])
    for kind in range(3):
        arrived(plane(y, core), send_y.at[kind])
    arrived(spectra.at[pl.ds(0, 63 * 16), :], send_a)
    own_beam.wait()
    arrived(formed.at[pl.ds(0, 127)], send_b)
    arrived(beams_ref.at[pl.ds(0, 127)], recv_b)


def finish_kernel(
    real_ref, imag_ref, beams_ref, high_hbm, low_hbm, real_hbm, imag_hbm, series_hbm,
    high_ref, low_ref, wide, turned, series, out_sem, load,
):
    loads = [
        pltpu.make_async_copy(high_hbm, high_ref, load.at[0]),
        pltpu.make_async_copy(low_hbm, low_ref, load.at[1]),
    ]
    for copy in loads:
        copy.start()
    copies = [
        pltpu.make_async_copy(real_ref, real_hbm.at[0, 0], out_sem.at[0]),
        pltpu.make_async_copy(imag_ref, imag_hbm.at[0, 0], out_sem.at[1]),
    ]
    for copy in copies:
        copy.start()
    for i in range(128):
        wide[i * 4 : (i + 1) * 4, :] = beams_ref[i].astype(jnp.float32)
    for h in range(2):
        for s in range(4):
            block = jnp.transpose(wide[pl.ds(h * 4 + s, 64, stride=8), :])
            for part in range(4):
                turned[h * 128 + s * 32 : h * 128 + (s + 1) * 32, part * 64 : (part + 1) * 64] = block[
                    part * 32 : (part + 1) * 32
                ].astype(jnp.bfloat16)
    for copy in loads:
        copy.wait()
    out = jnp.dot(turned[...], high_ref[...], preferred_element_type=jnp.float32)
    out += jnp.dot(turned[...], low_ref[...], preferred_element_type=jnp.float32)
    for h in range(2):
        for q in range(2):
            series[pl.ds(h * 256 + q, 128, stride=2), :] = out[
                h * 128 : (h + 1) * 128, q * 128 : (q + 1) * 128
            ]
    copies.append(pltpu.make_async_copy(series, series_hbm, out_sem.at[2]))
    copies[2].start()
    for copy in copies:
        copy.wait()


VMEM = pl.BlockSpec(memory_space=pltpu.VMEM)
HBM = pl.BlockSpec(memory_space=pltpu.HBM)


def in_hbm(array):
    return pltpu.with_memory_space_constraint(array, pltpu.HBM)


def per_device(voltages, slot_of_antenna, antenna_positions, beam_directions):
    high, low = forward_tables()
    real, imag, received = pl.pallas_call(
        kernel,
        out_shape=(
            jax.ShapeDtypeStruct((256, A), jnp.float32),
            jax.ShapeDtypeStruct((256, A), jnp.float32),
            jax.ShapeDtypeStruct((128, 4, 128), jnp.bfloat16),
        ),
        in_specs=[HBM] * 7,
        out_specs=(VMEM, VMEM, VMEM),
        scratch_shapes=[
            pltpu.VMEM((2, 16, 4096), jnp.bfloat16),
            pltpu.VMEM((256, 256), jnp.bfloat16),
            pltpu.VMEM((256, 256), jnp.bfloat16),
            pltpu.VMEM((16, 128), jnp.int32),
            pltpu.VMEM((2, A), jnp.int32),
            pltpu.VMEM((2, BEAMS), jnp.int32),
            pltpu.VMEM((1, 128), jnp.float32),
            pltpu.VMEM((2, 512, 128), jnp.float32),
            pltpu.VMEM((512, 256), jnp.bfloat16),
            pltpu.VMEM((1024, 128), jnp.float32),
            pltpu.VMEM((1024, 128), jnp.bfloat16),
            pltpu.VMEM((A, 512), jnp.bfloat16),
            pltpu.VMEM((A, A), jnp.bfloat16),
            pltpu.VMEM((256, A), jnp.bfloat16),
            pltpu.VMEM((256, A), jnp.bfloat16),
            pltpu.VMEM((A, 512), jnp.bfloat16),
            pltpu.VMEM((512, 512), jnp.bfloat16),
            pltpu.VMEM((512, 128), jnp.float32),
            pltpu.VMEM((128, 4, 128), jnp.bfloat16),
            pltpu.SemaphoreType.DMA,
            pltpu.SemaphoreType.DMA((16,)),
            pltpu.SemaphoreType.DMA((3,)),
            pltpu.SemaphoreType.DMA((3, 16)),
            pltpu.SemaphoreType.DMA((4,)),
            pltpu.SemaphoreType.DMA((4,)),
            pltpu.SemaphoreType.DMA,
            pltpu.SemaphoreType.DMA,
            pltpu.SemaphoreType.DMA,
            pltpu.SemaphoreType.DMA((7,)),
        ],
        compiler_params=pltpu.CompilerParams(
            collective_id=0, has_side_effects=True, vmem_limit_bytes=32 * 2**20
        ),
        name="correlator",
    )(
        *(
            in_hbm(array)
            for array in (
                voltages,
                jnp.asarray(high),
                jnp.asarray(low),
                slot_of_antenna.reshape(16, 128),
                antenna_positions.T,
                beam_directions.T,
                jnp.asarray(steering_table()),
            )
        )
    )
    inverse_high, inverse_low = inverse_tables()
    real, imag, series = pl.pallas_call(
        finish_kernel,
        out_shape=(
            jax.ShapeDtypeStruct((1, 1, 256, A), jnp.float32),
            jax.ShapeDtypeStruct((1, 1, 256, A), jnp.float32),
            jax.ShapeDtypeStruct((512, 128), jnp.float32),
        ),
        in_specs=[VMEM] * 3 + [HBM] * 2,
        out_specs=[HBM] * 3,
        scratch_shapes=[
            pltpu.VMEM((256, 256), jnp.bfloat16),
            pltpu.VMEM((256, 256), jnp.bfloat16),
            pltpu.VMEM((512, 128), jnp.float32),
            pltpu.VMEM((256, 256), jnp.bfloat16),
            pltpu.VMEM((512, 128), jnp.float32),
            pltpu.SemaphoreType.DMA((3,)),
            pltpu.SemaphoreType.DMA((2,)),
        ],
        compiler_params=pltpu.CompilerParams(vmem_limit_bytes=16 * 2**20),
        name="finish",
    )(
        real,
        imag,
        received,
        in_hbm(jnp.asarray(inverse_high)),
        in_hbm(jnp.asarray(inverse_low)),
    )
    series = series.reshape(2, 128, 2, 128).transpose(0, 2, 1, 3).reshape(2, 1, 1, 2, NB * 64)
    return (real, imag, series)


def solution(mesh):
    in_specs = (P(None, "band", "segment"), P(), P(), P())
    out_specs = (
        P("band", "segment", None, None),
        P("band", "segment", None, None),
        P(None, "segment", "band", None, None),
    )
    return jax.shard_map(
        per_device, mesh=mesh, in_specs=in_specs, out_specs=out_specs, check_vma=False
    )
```

time: 123 us -> 68.5 us (0.56)
  the two profiles are of different devices: /device:TPU:32 before, /device:TPU:1 now
where the time goes in v2:
time: 68.5 us; the launch traced here: 68.4 us
  Pallas kernels  67.7 us (99%)
    pallas_call x1, Pallas kernels, per_device(): pl.pallas_call(kernel, out_shape=(jax.ShapeDtypeStruct((256, A), jnp.floa...  65.5 us
    pallas_call x1, Pallas kernels, per_device(): pl.pallas_call(finish_kernel, out_shape=(jax.ShapeDtypeStruct((1, 1, 256,...  2.25 us

profile of v2, /device:TPU:1, one launch (start us, length us, event | category | flops | bytes accessed | tf_op | source)
XLA Modules:
  0.0 68.4 jit_solution(14765841006441522575)
XLA Ops:
  0.6 65.5 %correlator.1 = (f32[256,2048]{1,0:T(8,128)S(1)}, f32[256,2048]{1,0:T(8,128)S(1)}, bf16[128,4,128]{2,1,0:T(4,128)(2,1)S(1)}) custom-call(bf16[2,16,4096]{2,1,0:T(8,128)(2,1)} %v_hbm.1, bf16[256,256]{1,0:T(8,128)(2,1)} %constant.6.clone.high_hbm, bf16[256,256]{1,0:T(8,128)(2,1)} %constant.7.clone.low_hbm, s32[16,128]{1,0:T(8,128)} %bitcast.9, ...), custom_call_target="tpu_custom_call" | custom-call | tf_op jit(solution)/shard_map/correlator/pallas_call | solution.py:394
  66.1 2.3 %finish.1 = (f32[1,1,256,2048]{3,2,1,0:T(8,128)}, f32[1,1,256,2048]{3,2,1,0:T(8,128)}, f32[512,128]{1,0:T(8,128)}) custom-call(f32[256,2048]{1,0:T(8,128)S(1)} %get-tuple-element.9.real_ref, f32[256,2048]{1,0:T(8,128)S(1)} %get-tuple-element.10.imag_ref, bf16[128,4,128]{2,1,0:T(4,128)(2,1)S(1)} %get-tuple-element.11.beams_ref, ...), custom_call_target="tpu_custom_call" | custom-call | tf_op jit(solution)/shard_map/finish/pallas_call | solution.py:453

commit v3 on v2

--- a/solution.py
+++ b/solution.py
@@ -13,7 +13,8 @@
 BEAMS = 1024
 NB = 256
 MESH = pl.DeviceIdType.MESH
-LAG = 5
+LAG1 = 5
+LAG2 = 10
 
 
 def dft_parts():
@@ -61,7 +62,12 @@
 
 def offset_of(step):
     odd = step % 2
-    return (8 + odd * (-(step + 1) // 2) + (1 - odd) * (step // 2)) % 16
+    return (odd * ((step + 1) // 2) + (1 - odd) * (16 - step // 2)) % 16
+
+
+def far_offset(step):
+    odd = step % 2
+    return (8 - odd * ((step + 1) // 2) + (1 - odd) * (step // 2)) % 16
 
 
 def channelize(v_ref, high_ref, low_ref, wide, turned, spectra_f, spectra):
@@ -100,33 +106,22 @@
     return jnp.transpose(jnp.broadcast_to(row, (128, 128)))
 
 
-def build_pick(slot_ref, pick):
+def build_pick(slot_ref, pick, r):
     lane = lax.broadcasted_iota(jnp.int32, (128, 128), 1)
-
-    def block(r, carry):
-        slot = column_of(slot_ref[pl.ds(r, 1), :])
-        rows = pl.ds(pl.multiple_of(r * 128, 128), 128)
-        for c in range(16):
-            position = lane + c * 128
-            name = ((position % 1024) // 16) * 32 + (position // 1024) * 16 + position % 16
-            pick[rows, c * 128 : (c + 1) * 128] = jnp.where(slot == name, 1.0, 0.0).astype(
-                jnp.bfloat16
-            )
-        return carry
-
-    lax.fori_loop(0, 16, block, 0)
-
-
-def build_weights(pos_ref, dir_ref, tab_ref, weight_a, half, segment, channel):
-    start = pl.multiple_of(half * 512 + segment * 128, 128)
-    turn0 = column_of(dir_ref[0:1, pl.ds(start, 128)]) * channel
-    turn1 = column_of(dir_ref[1:2, pl.ds(start, 128)]) * channel
+    slot = column_of(slot_ref[pl.ds(r, 1), :])
+    rows = pl.ds(pl.multiple_of(r * 128, 128), 128)
+    for c in range(16):
+        position = lane + c * 128
+        name = ((position % 1024) // 16) * 32 + (position // 1024) * 16 + position % 16
+        pick[rows, c * 128 : (c + 1) * 128] = jnp.where(slot == name, 1.0, 0.0).astype(jnp.bfloat16)
+
+
+def build_weights(pos_ref, turn, tab_ref, weight_a, c):
     table = jnp.broadcast_to(tab_ref[...], (128, 128))
-    for c in range(16):
-        sl = slice(c * 128, (c + 1) * 128)
-        phase = (turn0 * pos_ref[0:1, sl] + turn1 * pos_ref[1:2, sl]) & 63
-        weight_a[0:128, sl] = jnp.take_along_axis(table, phase, axis=1).astype(jnp.bfloat16)
-        weight_a[128:256, sl] = jnp.take_along_axis(table, phase + 64, axis=1).astype(jnp.bfloat16)
+    lanes = pl.ds(pl.multiple_of(c * 128, 128), 128)
+    phase = (turn[0] * pos_ref[0:1, lanes] + turn[1] * pos_ref[1:2, lanes]) & 63
+    weight_a[0:128, lanes] = jnp.take_along_axis(table, phase, axis=1).astype(jnp.bfloat16)
+    weight_a[128:256, lanes] = jnp.take_along_axis(table, phase + 64, axis=1).astype(jnp.bfloat16)
 
 
 def kernel(
@@ -135,7 +130,7 @@
     v_ref, high_ref, low_ref, slot_ref, pos_ref, dir_ref, tab_ref,
     wide, turned, spectra_f, spectra, x_ref, pick, weight_a, weight_u, ordered, left,
     formed_f, formed,
-    send_a, recv_a, send_y, recv_y, send_c, recv_c, send_b, recv_b, own_b, load,
+    send_a, recv_a, send_y, recv_y, send_c, recv_c, send_b, recv_b, own_b, load, from_above, from_below,
 ):
     segment, band, core, half, channel, z, x, y = place()
     loads = [
@@ -162,23 +157,26 @@
     partner = column(y, 1 - core)
     barrier = pltpu.get_barrier_semaphore()
 
-    def greet(step, carry):
-        pl.semaphore_signal(
-            barrier, inc=1, device_id=(segment, (band + step) % 128), device_id_type=MESH
-        )
-        return carry
-
-    lax.fori_loop(1, 128, greet, 0)
-    for target in (column(up, core), column(down, core), partner):
+    above, below = ((z + 1) % 16) * 4 + x, ((z + 15) % 16) * 4 + x
+
+    def beside(other):
+        return (segment, other * 2 + half)
+
+    greeted = [beside(z * 4 + (x + across) % 4) for across in range(1, 4)]
+    greeted += [beside(above), beside(below), column(up, core), column(down, core), partner]
+    for target in greeted:
         pl.semaphore_signal(barrier, inc=1, device_id=target, device_id_type=MESH)
 
     for copy in loads:
         copy.wait()
     channelize(v_ref, high_ref, low_ref, wide, turned, spectra_f, spectra)
-    build_pick(slot_ref, pick)
-    build_weights(pos_ref, dir_ref, tab_ref, weight_a, half, segment, channel)
-
-    pl.semaphore_wait(barrier, 130)
+    pl.semaphore_wait(barrier, 8)
+
+    def tell(sem, target):
+        pl.semaphore_signal(sem, inc=1, device_id=beside(target), device_id_type=MESH)
+
+    tell(from_above, below)
+    tell(from_below, above)
 
     def chunk(y_from, core_from, z_from, rows):
         row = pl.multiple_of((y_from // 2) * 1024 + z_from * 64, 64)
@@ -201,27 +199,42 @@
             device_id_type=MESH,
         )
 
-    def send(step, carry):
-        for across in range(4):
-            message(step, across).start()
-        return carry
-
-    lax.fori_loop(0, 15, send, 0)
-    for across in range(1, 4):
-        message(15, across).start()
     own = pltpu.make_async_copy(
-        spectra.at[pl.ds(pl.multiple_of(channel * 16, 16), 16), :], home, recv_a.at[15]
+        spectra.at[pl.ds(pl.multiple_of(channel * 16, 16), 16), :], home, recv_a.at[0]
     )
     own.start()
-
-    def to_slots(c, carry):
+    for across in range(1, 4):
+        message(0, across).start()
+    start = pl.multiple_of(half * 512 + segment * 128, 128)
+    turn = [column_of(dir_ref[i : i + 1, pl.ds(start, 128)]) * channel for i in range(2)]
+
+    def reach(d, carry):
+        pl.semaphore_wait(from_above, 1)
+        tell(from_above, below)
+        for across in range(4):
+            message(2 * d - 1, across).start()
+        pl.semaphore_wait(from_below, 1)
+        pl.when(d < 7)(lambda: tell(from_below, above))
+        for across in range(4):
+            message(2 * d, across).start()
+        for i in range(2):
+            build_pick(slot_ref, pick, 2 * d - 2 + i)
+            build_weights(pos_ref, turn, tab_ref, weight_a, 2 * d - 2 + i)
+        return carry
+
+    lax.fori_loop(1, 8, reach, 0)
+    pl.semaphore_wait(from_above, 1)
+    for across in range(4):
+        message(15, across).start()
+    for i in range(14, 16):
+        build_pick(slot_ref, pick, i)
+        build_weights(pos_ref, turn, tab_ref, weight_a, i)
+
+    def to_slots(c):
         lanes = pl.ds(pl.multiple_of(c * 256, 256), 256)
         weight_u[:, lanes] = jnp.dot(
             weight_a[...], pick[:, lanes], preferred_element_type=jnp.float32
         ).astype(jnp.bfloat16)
-        return carry
-
-    lax.fori_loop(0, 8, to_slots, 0)
 
     def forward(y_from, step, target, send_sem, recv_sem):
         source = chunk(y_from, core, (z + 16 - offset_of(step)) % 16, 64)
@@ -263,11 +276,12 @@
 
     def body(step, carry):
         pl.when(step < 16)(lambda: level0(step))
-        pl.when((step >= LAG) & (step < 16 + LAG))(lambda: level1(step - LAG))
-        pl.when(step >= 2 * LAG)(lambda: level2(step - 2 * LAG))
+        pl.when((step >= LAG1) & (step < 16 + LAG1))(lambda: level1(step - LAG1))
+        pl.when(step >= LAG2)(lambda: level2(step - LAG2))
+        pl.when((step >= 4) & (step < 12))(lambda: to_slots(step - 4))
         return carry
 
-    lax.fori_loop(0, 16 + 2 * LAG, body, 0)
+    lax.fori_loop(0, 16 + LAG2, body, 0)
 
     def plane(y_from, core_from):
         return chunk(y_from, core_from, 0, 1024)
@@ -286,8 +300,8 @@
     for e in range(128):
         formed[e] = formed_f[e * 4 : (e + 1) * 4, :].astype(jnp.bfloat16)
 
-    def send_beams(step, carry):
-        to = (band + 64 + step) % 128
+    def send_beam(step, turn_by):
+        to = ((z + far_offset(step)) % 16) * 8 + (band % 8 + turn_by) % 8
         pltpu.make_async_remote_copy(
             src_ref=formed.at[to],
             dst_ref=beams_ref.at[band],
@@ -296,10 +310,15 @@
             device_id=(segment, to),
             device_id_type=MESH,
         ).start()
+
+    def send_beams(step, carry):
+        for turn_by in range(8):
+            send_beam(step, turn_by)
         return carry
 
-    lax.fori_loop(0, 64, send_beams, 0)
-    lax.fori_loop(65, 128, send_beams, 0)
+    lax.fori_loop(0, 15, send_beams, 0)
+    for turn_by in range(1, 8):
+        send_beam(15, turn_by)
     own_beam = pltpu.make_async_copy(formed.at[band], beams_ref.at[band], own_b)
     own_beam.start()
 
@@ -430,6 +449,8 @@
             pltpu.SemaphoreType.DMA,
             pltpu.SemaphoreType.DMA,
             pltpu.SemaphoreType.DMA((7,)),
+            pltpu.SemaphoreType.REGULAR,
+            pltpu.SemaphoreType.REGULAR,
         ],
         compiler_params=pltpu.CompilerParams(
             collective_id=0, has_side_effects=True, vmem_limit_bytes=32 * 2**20

time: 68.5 us -> 57.2 us (0.84)
  Pallas kernels: 67.7 us -> 56.4 us
    pallas_call x1, Pallas kernels: 65.5 us -> 54.2 us  [per_device(): pl.pallas_call(kernel, out_shape=(jax.ShapeDtypeStruct((256, A), jnp.floa...]
where the time goes in v3:
time: 57.2 us; the launch traced here: 57 us
  Pallas kernels  56.4 us (99%)
  between operations  0.64 us (1%)
    pallas_call x1, Pallas kernels, per_device(): pl.pallas_call(kernel, out_shape=(jax.ShapeDtypeStruct((256, A), jnp.floa...  54.2 us
    pallas_call x1, Pallas kernels, per_device(): pl.pallas_call(finish_kernel, out_shape=(jax.ShapeDtypeStruct((1, 1, 256,...  2.25 us

profile of v3, /device:TPU:1, one launch (start us, length us, event | category | flops | bytes accessed | tf_op | source)
XLA Modules:
  0.0 57.0 jit_solution(4224303964837837135)
XLA Ops:
  0.6 54.2 %correlator.1 = (f32[256,2048]{1,0:T(8,128)S(1)}, f32[256,2048]{1,0:T(8,128)S(1)}, bf16[128,4,128]{2,1,0:T(4,128)(2,1)S(1)}) custom-call(bf16[2,16,4096]{2,1,0:T(8,128)(2,1)} %v_hbm.1, bf16[256,256]{1,0:T(8,128)(2,1)} %constant.6.clone.high_hbm, bf16[256,256]{1,0:T(8,128)(2,1)} %constant.7.clone.low_hbm, s32[16,128]{1,0:T(8,128)} %bitcast.9, ...), custom_call_target="tpu_custom_call" | custom-call | tf_op jit(solution)/shard_map/correlator/pallas_call | solution.py:413
  54.8 2.2 %finish.1 = (f32[1,1,256,2048]{3,2,1,0:T(8,128)}, f32[1,1,256,2048]{3,2,1,0:T(8,128)}, f32[512,128]{1,0:T(8,128)}) custom-call(f32[256,2048]{1,0:T(8,128)S(1)} %get-tuple-element.9.real_ref, f32[256,2048]{1,0:T(8,128)S(1)} %get-tuple-element.10.imag_ref, bf16[128,4,128]{2,1,0:T(4,128)(2,1)S(1)} %get-tuple-element.11.beams_ref, ...), custom_call_target="tpu_custom_call" | custom-call | tf_op jit(solution)/shard_map/finish/pallas_call | solution.py:474

commit v4 on v3

--- a/solution.py
+++ b/solution.py
@@ -13,8 +13,12 @@
 BEAMS = 1024
 NB = 256
 MESH = pl.DeviceIdType.MESH
-LAG1 = 5
-LAG2 = 10
+LAG1 = 8
+LAG2 = 8
+NEAR = 7
+FAR = 2 * NEAR + 1
+DIRECT = 0
+BOTH = 13
 
 
 def dft_parts():
@@ -60,7 +64,7 @@
     return segment, band, core, half, channel, channel // 4, channel % 4, half * 2 + segment // 2
 
 
-def offset_of(step):
+def near_offset(step):
     odd = step % 2
     return (odd * ((step + 1) // 2) + (1 - odd) * (16 - step // 2)) % 16
 
@@ -68,6 +72,10 @@
 def far_offset(step):
     odd = step % 2
     return (8 - odd * ((step + 1) // 2) + (1 - odd) * (step // 2)) % 16
+
+
+def offset_of(step):
+    return jnp.where(step < FAR, near_offset(step), far_offset(jnp.maximum(step - FAR, 0)))
 
 
 def channelize(v_ref, high_ref, low_ref, wide, turned, spectra_f, spectra):
@@ -164,13 +172,15 @@
 
     greeted = [beside(z * 4 + (x + across) % 4) for across in range(1, 4)]
     greeted += [beside(above), beside(below), column(up, core), column(down, core), partner]
+    greeted += [column((y + 2) % 4, core), column((y + 2) % 4, 1 - core)]
+    greeted += [column(up, 1 - core), column(down, 1 - core)]
     for target in greeted:
         pl.semaphore_signal(barrier, inc=1, device_id=target, device_id_type=MESH)
 
     for copy in loads:
         copy.wait()
     channelize(v_ref, high_ref, low_ref, wide, turned, spectra_f, spectra)
-    pl.semaphore_wait(barrier, 8)
+    pl.semaphore_wait(barrier, 12)
 
     def tell(sem, target):
         pl.semaphore_signal(sem, inc=1, device_id=beside(target), device_id_type=MESH)
@@ -211,24 +221,32 @@
     def reach(d, carry):
         pl.semaphore_wait(from_above, 1)
         tell(from_above, below)
-        for across in range(4):
-            message(2 * d - 1, across).start()
         pl.semaphore_wait(from_below, 1)
         pl.when(d < 7)(lambda: tell(from_below, above))
-        for across in range(4):
-            message(2 * d, across).start()
-        for i in range(2):
-            build_pick(slot_ref, pick, 2 * d - 2 + i)
-            build_weights(pos_ref, turn, tab_ref, weight_a, 2 * d - 2 + i)
+
+        @pl.when(d <= NEAR)
+        def _():
+            for across in range(4):
+                message(2 * d - 1, across).start()
+            for across in range(4):
+                message(2 * d, across).start()
+
         return carry
 
     lax.fori_loop(1, 8, reach, 0)
     pl.semaphore_wait(from_above, 1)
-    for across in range(4):
-        message(15, across).start()
-    for i in range(14, 16):
-        build_pick(slot_ref, pick, i)
-        build_weights(pos_ref, turn, tab_ref, weight_a, i)
+
+    def send_far(step, carry):
+        for across in range(4):
+            message(step, across).start()
+        return carry
+
+    lax.fori_loop(FAR, 16, send_far, 0)
+
+    def prepare(step):
+        for i in range(2):
+            build_pick(slot_ref, pick, 2 * step + i)
+            build_weights(pos_ref, turn, tab_ref, weight_a, 2 * step + i)
 
     def to_slots(c):
         lanes = pl.ds(pl.multiple_of(c * 256, 256), 256)
@@ -263,22 +281,44 @@
         forward(y, step, column(down, core), send_y.at[1], recv_y.at[1, step]).start()
         to_partner(y, 0, step)
 
+        @pl.when(step >= DIRECT)
+        def _():
+            forward(
+                y, step, column(across_from, core), send_y.at[2], recv_y.at[2, step]
+            ).start()
+
+        @pl.when(step >= BOTH)
+        def _():
+            for kind, y_to in ((1, up), (2, down), (3, across_from)):
+                forward(
+                    y, step, column(y_to, 1 - core), send_c.at[kind], recv_c.at[kind]
+                ).start()
+
     def level1(step):
         forward(down, step, partner, send_y.at[0], recv_y.at[0, step]).wait_recv()
         forward(up, step, partner, send_y.at[1], recv_y.at[1, step]).wait_recv()
-        forward(relay_from, step, column(relay_to, core), send_y.at[2], recv_y.at[2, step]).start()
-        to_partner(down, 1, step)
-        to_partner(up, 2, step)
+        @pl.when(step < DIRECT)
+        def _():
+            forward(
+                relay_from, step, column(relay_to, core), send_y.at[2], recv_y.at[2, step]
+            ).start()
+
+        @pl.when(step < BOTH)
+        def _():
+            to_partner(down, 1, step)
+            to_partner(up, 2, step)
+
 
     def level2(step):
         forward(across_from, step, partner, send_y.at[2], recv_y.at[2, step]).wait_recv()
-        to_partner(across_from, 3, step)
+        pl.when(step < BOTH)(lambda: to_partner(across_from, 3, step))
 
     def body(step, carry):
         pl.when(step < 16)(lambda: level0(step))
         pl.when((step >= LAG1) & (step < 16 + LAG1))(lambda: level1(step - LAG1))
         pl.when(step >= LAG2)(lambda: level2(step - LAG2))
-        pl.when((step >= 4) & (step < 12))(lambda: to_slots(step - 4))
+        pl.when(step < 8)(lambda: prepare(step))
+        pl.when((step >= 8) & (step < 16))(lambda: to_slots(step - 8))
         return carry
 
     lax.fori_loop(0, 16 + LAG2, body, 0)

time: 57.2 us -> 54.1 us (0.946)
  Pallas kernels: 56.4 us -> 53.3 us
    pallas_call x1, Pallas kernels: 54.2 us -> 51.1 us  [per_device(): pl.pallas_call(kernel, out_shape=(jax.ShapeDtypeStruct((256, A), jnp.floa...]
where the time goes in v4:
time: 54.1 us; the launch traced here: 54 us
  Pallas kernels  53.3 us (99%)
  between operations  0.64 us (1%)
    pallas_call x1, Pallas kernels, per_device(): pl.pallas_call(kernel, out_shape=(jax.ShapeDtypeStruct((256, A), jnp.floa...  51.1 us
    pallas_call x1, Pallas kernels, per_device(): pl.pallas_call(finish_kernel, out_shape=(jax.ShapeDtypeStruct((1, 1, 256,...  2.25 us

profile of v4, /device:TPU:1, one launch (start us, length us, event | category | flops | bytes accessed | tf_op | source)
XLA Modules:
  0.0 54.0 jit_solution(157763723098934154)
XLA Ops:
  0.6 51.1 %correlator.1 = (f32[256,2048]{1,0:T(8,128)S(1)}, f32[256,2048]{1,0:T(8,128)S(1)}, bf16[128,4,128]{2,1,0:T(4,128)(2,1)S(1)}) custom-call(bf16[2,16,4096]{2,1,0:T(8,128)(2,1)} %v_hbm.1, bf16[256,256]{1,0:T(8,128)(2,1)} %constant.6.clone.high_hbm, bf16[256,256]{1,0:T(8,128)(2,1)} %constant.7.clone.low_hbm, s32[16,128]{1,0:T(8,128)} %bitcast.9, ...), custom_call_target="tpu_custom_call" | custom-call | tf_op jit(solution)/shard_map/correlator/pallas_call | solution.py:453
  51.7 2.3 %finish.1 = (f32[1,1,256,2048]{3,2,1,0:T(8,128)}, f32[1,1,256,2048]{3,2,1,0:T(8,128)}, f32[512,128]{1,0:T(8,128)}) custom-call(f32[256,2048]{1,0:T(8,128)S(1)} %get-tuple-element.9.real_ref, f32[256,2048]{1,0:T(8,128)S(1)} %get-tuple-element.10.imag_ref, bf16[128,4,128]{2,1,0:T(4,128)(2,1)S(1)} %get-tuple-element.11.beams_ref, ...), custom_call_target="tpu_custom_call" | custom-call | tf_op jit(solution)/shard_map/finish/pallas_call | solution.py:514

commit v5 on v4

--- a/solution.py
+++ b/solution.py
@@ -15,10 +15,10 @@
 MESH = pl.DeviceIdType.MESH
 LAG1 = 8
 LAG2 = 8
-NEAR = 7
+NEAR = 6
 FAR = 2 * NEAR + 1
 DIRECT = 0
-BOTH = 13
+BOTH = 14
 
 
 def dft_parts():
@@ -198,8 +198,10 @@
         pl.ds(pl.multiple_of(segment * 128, 128), 128),
     ]
 
-    def message(step, across):
-        to = ((z + offset_of(step)) % 16) * 4 + (x + across) % 4
+    columns = [(x + across) % 4 for across in range(4)]
+
+    def message(step, across, base):
+        to = base + columns[across]
         return pltpu.make_async_remote_copy(
             src_ref=spectra.at[pl.ds(pl.multiple_of(to * 16, 16), 16), :],
             dst_ref=home,
@@ -214,7 +216,13 @@
     )
     own.start()
     for across in range(1, 4):
-        message(0, across).start()
+        message(0, across, z * 4).start()
+
+    def messages(step):
+        base = ((z + offset_of(step)) % 16) * 4
+        for across in range(4):
+            message(step, across, base).start()
+
     start = pl.multiple_of(half * 512 + segment * 128, 128)
     turn = [column_of(dir_ref[i : i + 1, pl.ds(start, 128)]) * channel for i in range(2)]
 
@@ -226,10 +234,8 @@
 
         @pl.when(d <= NEAR)
         def _():
-            for across in range(4):
-                message(2 * d - 1, across).start()
-            for across in range(4):
-                message(2 * d, across).start()
+            messages(2 * d - 1)
+            messages(2 * d)
 
         return carry
 
@@ -237,8 +243,7 @@
     pl.semaphore_wait(from_above, 1)
 
     def send_far(step, carry):
-        for across in range(4):
-            message(step, across).start()
+        messages(step)
         return carry
 
     lax.fori_loop(FAR, 16, send_far, 0)
@@ -340,8 +345,9 @@
     for e in range(128):
         formed[e] = formed_f[e * 4 : (e + 1) * 4, :].astype(jnp.bfloat16)
 
-    def send_beam(step, turn_by):
-        to = ((z + far_offset(step)) % 16) * 8 + (band % 8 + turn_by) % 8
+    lows = [(band % 8 + turn_by) % 8 for turn_by in range(8)]
+
+    def send_beam(to):
         pltpu.make_async_remote_copy(
             src_ref=formed.at[to],
             dst_ref=beams_ref.at[band],
@@ -352,13 +358,14 @@
         ).start()
 
     def send_beams(step, carry):
-        for turn_by in range(8):
-            send_beam(step, turn_by)
+        base = ((z + far_offset(step)) % 16) * 8
+        for low in lows:
+            send_beam(base + low)
         return carry
 
     lax.fori_loop(0, 15, send_beams, 0)
-    for turn_by in range(1, 8):
-        send_beam(15, turn_by)
+    for low in lows[1:]:
+        send_beam(z * 8 + low)
     own_beam = pltpu.make_async_copy(formed.at[band], beams_ref.at[band], own_b)
     own_beam.start()
 

time: 54.1 us -> 53.9 us (level)
  no operation moved by 1% of the time
where the time goes in v5:
time: 53.9 us; the launch traced here: 53.7 us
  Pallas kernels  53.1 us (99%)
  between operations  0.64 us (1%)
    pallas_call x1, Pallas kernels, per_device(): pl.pallas_call(kernel, out_shape=(jax.ShapeDtypeStruct((256, A), jnp.floa...  50.8 us
    pallas_call x1, Pallas kernels, per_device(): pl.pallas_call(finish_kernel, out_shape=(jax.ShapeDtypeStruct((1, 1, 256,...  2.25 us

profile of v5, /device:TPU:1, one launch (start us, length us, event | category | flops | bytes accessed | tf_op | source)
XLA Modules:
  0.0 53.7 jit_solution(8129492709537660628)
XLA Ops:
  0.6 50.8 %correlator.1 = (f32[256,2048]{1,0:T(8,128)S(1)}, f32[256,2048]{1,0:T(8,128)S(1)}, bf16[128,4,128]{2,1,0:T(4,128)(2,1)S(1)}) custom-call(bf16[2,16,4096]{2,1,0:T(8,128)(2,1)} %v_hbm.1, bf16[256,256]{1,0:T(8,128)(2,1)} %constant.6.clone.high_hbm, bf16[256,256]{1,0:T(8,128)(2,1)} %constant.7.clone.low_hbm, s32[16,128]{1,0:T(8,128)} %bitcast.9, ...), custom_call_target="tpu_custom_call" | custom-call | tf_op jit(solution)/shard_map/correlator/pallas_call | solution.py:460
  51.5 2.3 %finish.1 = (f32[1,1,256,2048]{3,2,1,0:T(8,128)}, f32[1,1,256,2048]{3,2,1,0:T(8,128)}, f32[512,128]{1,0:T(8,128)}) custom-call(f32[256,2048]{1,0:T(8,128)S(1)} %get-tuple-element.9.real_ref, f32[256,2048]{1,0:T(8,128)S(1)} %get-tuple-element.10.imag_ref, bf16[128,4,128]{2,1,0:T(4,128)(2,1)S(1)} %get-tuple-element.11.beams_ref, ...), custom_call_target="tpu_custom_call" | custom-call | tf_op jit(solution)/shard_map/finish/pallas_call | solution.py:521

commit v6 on v5

--- a/solution.py
+++ b/solution.py
@@ -418,8 +418,11 @@
     for copy in loads:
         copy.start()
     copies = [
-        pltpu.make_async_copy(real_ref, real_hbm.at[0, 0], out_sem.at[0]),
-        pltpu.make_async_copy(imag_ref, imag_hbm.at[0, 0], out_sem.at[1]),
+        pltpu.make_async_copy(
+            source.at[pl.ds(i * 64, 64)], target.at[0, 0, pl.ds(i * 64, 64)], out_sem.at[n * 4 + i]
+        )
+        for n, (source, target) in enumerate(((real_ref, real_hbm), (imag_ref, imag_hbm)))
+        for i in range(4)
     ]
     for copy in copies:
         copy.start()
@@ -441,8 +444,8 @@
             series[pl.ds(h * 256 + q, 128, stride=2), :] = out[
                 h * 128 : (h + 1) * 128, q * 128 : (q + 1) * 128
             ]
-    copies.append(pltpu.make_async_copy(series, series_hbm, out_sem.at[2]))
-    copies[2].start()
+    copies.append(pltpu.make_async_copy(series, series_hbm, out_sem.at[8]))
+    copies[8].start()
     for copy in copies:
         copy.wait()
 
@@ -533,7 +536,7 @@
             pltpu.VMEM((512, 128), jnp.float32),
             pltpu.VMEM((256, 256), jnp.bfloat16),
             pltpu.VMEM((512, 128), jnp.float32),
-            pltpu.SemaphoreType.DMA((3,)),
+            pltpu.SemaphoreType.DMA((9,)),
             pltpu.SemaphoreType.DMA((2,)),
         ],
         compiler_params=pltpu.CompilerParams(vmem_limit_bytes=16 * 2**20),

time: 53.9 us -> 54.1 us (level)
  no operation moved by 1% of the time
where the time goes in v6:
time: 54.1 us; the launch traced here: 53.9 us
  Pallas kernels  53.2 us (98%)
  between operations  0.64 us (1%)
    pallas_call x1, Pallas kernels, per_device(): pl.pallas_call(kernel, out_shape=(jax.ShapeDtypeStruct((256, A), jnp.floa...  50.8 us
    pallas_call x1, Pallas kernels, per_device(): pl.pallas_call(finish_kernel, out_shape=(jax.ShapeDtypeStruct((1, 1, 256,...  2.4 us

profile of v6, /device:TPU:1, one launch (start us, length us, event | category | flops | bytes accessed | tf_op | source)
XLA Modules:
  0.0 53.9 jit_solution(6899453960995241685)
XLA Ops:
  0.6 50.8 %correlator.1 = (f32[256,2048]{1,0:T(8,128)S(1)}, f32[256,2048]{1,0:T(8,128)S(1)}, bf16[128,4,128]{2,1,0:T(4,128)(2,1)S(1)}) custom-call(bf16[2,16,4096]{2,1,0:T(8,128)(2,1)} %v_hbm.1, bf16[256,256]{1,0:T(8,128)(2,1)} %constant.6.clone.high_hbm, bf16[256,256]{1,0:T(8,128)(2,1)} %constant.7.clone.low_hbm, s32[16,128]{1,0:T(8,128)} %bitcast.9, ...), custom_call_target="tpu_custom_call" | custom-call | tf_op jit(solution)/shard_map/correlator/pallas_call | solution.py:463
  51.5 2.4 %finish.1 = (f32[1,1,256,2048]{3,2,1,0:T(8,128)}, f32[1,1,256,2048]{3,2,1,0:T(8,128)}, f32[512,128]{1,0:T(8,128)}) custom-call(f32[256,2048]{1,0:T(8,128)S(1)} %get-tuple-element.9.real_ref, f32[256,2048]{1,0:T(8,128)S(1)} %get-tuple-element.10.imag_ref, bf16[128,4,128]{2,1,0:T(4,128)(2,1)S(1)} %get-tuple-element.11.beams_ref, ...), custom_call_target="tpu_custom_call" | custom-call | tf_op jit(solution)/shard_map/finish/pallas_call | solution.py:524
